TPU v7x, 128 devices: a whole 4x4x4 slice. The times are simulated.
128 devices in a mesh: grp: 4 (over y), dev: 32 (over z, x, core).
Axes of the slice: x: 4, y: 4, z: 4, core: 2. Of those that a mesh axis runs over, the one named last changes fastest.
Arguments:
- points: float32 [3, 65536], P(None, 'dev'), may hold values from 0 to 1
- omega: bfloat16 [65536, 256], P('dev'), may hold values from -0.0234375 to 0.0234375
- pivots: int32 [32, 256], replicated, may hold values from 0 to 2047, as said below
- ranks: int32 [32], replicated, may hold values from 128 to 256, as said below
- owners: int32 [16], replicated, may hold values from 0 to 3, as said below
Outputs:
- interp: float32 [65536, 256], P(('grp', 'dev'))
- parent_samples: float32 [4, 8, 512, 256], P('grp', None, 'dev')
Inputs may be any that keep to these rules, and one draw needn't show every extreme that they name: The 256 pivots of a leaf are distinct. `ranks`: some leaf has exactly 256 skeleton rows in every draw. `owners`: no owner holds more than 8 parents, and some owner holds exactly 8.
All inputs are finite; a program needn't handle non-finite values.
Results may differ from a plain program's by a relative error of at most 0.0097.
Values may be sent and summed in bfloat16 or wider, within the bound.
A program may use at most 192 MiB of HBM per device.

v0:
```python
import math
import jax
import jax.numpy as jnp
from jax import lax
from jax.sharding import PartitionSpec as P

soften = 0.0001
highest = lax.Precision.HIGHEST


def copy_for_each(value, axis):
    copies = jnp.broadcast_to(value, (lax.axis_size(axis), *value.shape))
    return lax.all_to_all(copies, axis, split_axis=0, concat_axis=0, tiled=True)


def joined_along(parts, dim):
    parts = jnp.moveaxis(parts, 0, dim)
    lengths = parts.shape
    return parts.reshape(*lengths[:dim], lengths[dim] * lengths[dim + 1], *lengths[dim + 2 :])


def gathered_copies(value, axis, dim):
    parts = copy_for_each(value, axis)
    return joined_along(parts, dim)


def in_blocks(value, dim, peers):
    before, after = (value.shape[:dim], value.shape[dim + 1 :])
    return jnp.moveaxis(value.reshape(*before, peers, -1, *after), dim, 0)


def sum_at_owner(value, axis, dim):
    parts = in_blocks(value, dim, lax.axis_size(axis))
    arrived = lax.all_to_all(parts, axis, split_axis=0, concat_axis=0, tiled=True)
    return arrived.sum(axis=0)


def shifted(block, axis, distance):
    devices = range(lax.axis_size(axis))
    route = [(i - distance, i) for i in devices if i - distance in devices]
    return lax.ppermute(block, axis, route)


def kernel_block(row_pts, col_pts):
    dist_sq = (row_pts[0][:, None] - col_pts[0][None, :]) ** 2
    dist_sq = dist_sq + (row_pts[1][:, None] - col_pts[1][None, :]) ** 2
    dist_sq = dist_sq + (row_pts[2][:, None] - col_pts[2][None, :]) ** 2
    return 1.0 / jnp.sqrt(dist_sq + soften)


def body(points, omega, pivots, ranks, owners):
    groups = lax.axis_size("grp")
    devices = lax.axis_size("dev")
    group_id = lax.axis_index("grp")
    device_id = lax.axis_index("dev")
    leaf_size = omega.shape[0]
    samples_n = omega.shape[1]
    rank_max = pivots.shape[1]
    count_all = leaf_size * devices
    rows_group = count_all // groups
    slab_rows = leaf_size // groups
    leaves_group = devices // groups
    every_point = gathered_copies(points, "dev", 1)
    slab_start = group_id * rows_group + device_id * slab_rows
    my_leaf = slab_start // leaf_size
    slab_pts = lax.dynamic_slice_in_dim(every_point, slab_start, slab_rows, 1)
    start_sum = jnp.zeros((slab_rows, samples_n), jnp.float32)
    piece = lax.all_gather(omega, "dev", axis=0, tiled=True)
    piece_len = piece.shape[0]
    col_blk = math.gcd(piece_len, 2048)

    def one_block(number, running):
        first_col = number * col_blk
        col_pts = lax.dynamic_slice_in_dim(every_point, first_col, col_blk, 1)
        sketch = lax.dynamic_slice_in_dim(piece, number * col_blk, col_blk, 0)
        col_leaf = (first_col + jnp.arange(col_blk, dtype=jnp.int32)) // leaf_size
        kernel = kernel_block(slab_pts, col_pts)
        kernel = jnp.where(col_leaf[None, :] == my_leaf, 0.0, kernel).astype(jnp.bfloat16)
        return running + jnp.dot(kernel, sketch, preferred_element_type=jnp.float32)

    slab_samples = lax.fori_loop(0, piece_len // col_blk, one_block, start_sum)
    rank_ids = jnp.arange(rank_max, dtype=jnp.int32)
    local_leaf = device_id // groups
    within = slab_start - my_leaf * leaf_size
    my_pivots = pivots[my_leaf]
    my_live = rank_ids < ranks[my_leaf]
    slab_ids = jnp.arange(slab_rows, dtype=jnp.int32)
    picker = (my_pivots[:, None] - within == slab_ids[None, :]) & my_live[:, None]
    picked = jnp.dot(picker.astype(jnp.float32), slab_samples, precision=highest)
    sibling_leaf = jnp.bitwise_xor(device_id, 1)
    sib_pivots = pivots[sibling_leaf]
    sib_pts = every_point[:, sibling_leaf * leaf_size + sib_pivots]
    sib_kernel = kernel_block(sib_pts, points).astype(jnp.bfloat16)
    sib_live = (rank_ids < ranks[sibling_leaf]) & (device_id // leaves_group == group_id)
    correction = jnp.where(
        sib_live[:, None], jnp.dot(sib_kernel, omega, preferred_element_type=jnp.float32), 0.0
    )
    leaf_slots = jnp.arange(leaves_group, dtype=jnp.int32)
    skel_all = jnp.where((leaf_slots == local_leaf)[:, None, None], picked[None], 0.0)
    corr_all = jnp.where(
        (leaf_slots == sibling_leaf - group_id * leaves_group)[:, None, None], correction[None], 0.0
    )
    pairs_group = leaves_group // 2
    paired_part = (skel_all - corr_all).reshape(pairs_group, 2 * rank_max, samples_n)
    my_piece = sum_at_owner(paired_part, "dev", 1)
    position = device_id % groups
    skel_rows = picked
    for offset in range(1 - groups, groups):
        if offset != 0:
            arrived = shifted(picked, "dev", offset)
            source = position - offset
            skel_rows = skel_rows + jnp.where((source >= 0) & (source < groups), arrived, 0.0)
    gram_mat = jnp.dot(skel_rows, skel_rows.T, precision=highest)
    ridge_term = 0.1 * jnp.trace(gram_mat) / ranks[my_leaf].astype(jnp.float32) + 1e-06
    gram_mat = gram_mat + ridge_term * jnp.eye(rank_max, dtype=jnp.float32)
    factor = jnp.linalg.cholesky(gram_mat)
    right_side = jnp.dot(slab_samples, skel_rows.T, precision=highest)
    interp = jax.scipy.linalg.cho_solve((factor, True), right_side.T).T
    parent_count = owners.shape[0]
    slot_count = 2 * pairs_group
    parent_ids = jnp.arange(parent_count, dtype=jnp.int32)
    shared = owners[:, None] == owners[None, :]
    slot_of = jnp.sum(shared & (parent_ids[None, :] < parent_ids[:, None]), axis=1)
    slot_ids = jnp.arange(slot_count, dtype=jnp.int32)
    all_pieces = lax.all_gather(my_piece, "grp", axis=0, tiled=True)
    placing = (owners[None, :] == group_id) & (slot_ids[:, None] == slot_of[None, :])
    delivered = jnp.einsum(
        "sp,prk->srk", placing.astype(jnp.float32), all_pieces, precision=highest
    )
    return (interp, delivered[None])


def solution(mesh):
    placed = (P(None, "dev"), P("dev", None), P(), P(), P())
    return jax.shard_map(
        body,
        mesh=mesh,
        in_specs=placed,
        out_specs=(P(("grp", "dev"), None), P("grp", None, "dev", None)),
        check_vma=False,
    )
```

profile of v0, /device:TPU:33, one launch (start us, length us, event | category | flops | bytes accessed | tf_op | source)
XLA Modules:
  0.0 352.9 jit_solution(2332731837905459463)
XLA Ops:
  9.9 8.3 %all-to-all-start = ((f32[32,3,2048]{2,1,0:T(4,128)}), f32[32,3,2048]{2,1,0:T(4,128)S(1)}, u32[]{:S(2)}, u32[]{:S(2)}) async-start(f32[32,3,2048]{2,1,0:T(4,128)} %broadcast_in_dim.127), calls=%async_computation | async-start | bytes 2097152 | tf_op jit(solution)/shard_map/all_to_all | solution.py:13
  23.4 16.6 %all-to-all-done = f32[32,3,2048]{2,1,0:T(4,128)S(1)} async-done(((f32[32,3,2048]{2,1,0:T(4,128)}), f32[32,3,2048]{2,1,0:T(4,128)S(1)}, u32[]{:S(2)}, u32[]{:S(2)}) %all-to-all-start) | async-done | bytes 786464 | tf_op jit(solution)/shard_map/all_to_all | solution.py:13
  39.9 15.4 %copy.36 = f32[3,32,2048]{0,2,1:T(8,128)} copy(f32[3,32,2048]{2,0,1:T(4,128)S(1)} %bitcast.89) | data formatting | bytes 1572864 | tf_op jit(solution)/shard_map/transpose | solution.py:17
  55.3 20.0 %copy.38 = f32[3,65536]{1,0:T(4,128)S(1)} copy(f32[3,65536]{0,1:T(8,128)} %bitcast.84) | data formatting | bytes 1572864
  75.3 12.7 %gather_fusion = f32[256,3]{1,0:T(8,128)S(1)} fusion(f32[3,65536]{0,1:T(8,128)} %bitcast.85, s32[1024]{0:T(1024)S(1)} %pad_clamp_fusion), kind=kCustom, calls=%fused_computation | custom fusion | bytes 7168 | tf_op jit(solution)/shard_map/gather | solution.py:92
  89.4 41.9 %all-gather.2.cloned.1.call-done = bf16[65536,256]{1,0:T(8,128)(2,1)} async-done(((bf16[2048,256]{1,0:T(8,128)(2,1)}), bf16[65536,256]{1,0:T(8,128)(2,1)}) %all-gather.2.cloned.1.call-update) | async-done | bytes 33554448 | tf_op jit(solution)/shard_map/all_gather | solution.py:68
  131.2 98.0 %while.18 = (s32[]{:T(128)}, f32[512,256]{1,0:T(8,128)S(1)}, s32[]{:T(128)}, f32[3,512]{1,0:T(4,128)S(1)}, f32[3,65536]{1,0:T(4,128)S(1)}, /*index=5*/bf16[65536...) while((s32[]{:T(128)}, f32[512,256]{1,0:T(8,128)S(1)}, ...), condition=%wide.region_1.2_spmd.clone, body=%wide.region_0.1_spmd.clone.sunk | while | flops 548702208 | bytes 2193629 | solution.py:81
  131.4 3.0 fusion.72
  134.5 2.9 fusion.72
  137.6 2.9 fusion.72
  143.7 2.9 fusion.72
  146.7 2.9 fusion.72
  149.8 2.9 fusion.72
  155.9 2.9 fusion.72
  159.0 2.9 fusion.72
  165.1 2.9 fusion.72
  177.3 2.9 fusion.72
  180.4 2.9 fusion.72
  186.5 2.9 fusion.72
  198.8 2.9 fusion.72
  211.0 2.9 fusion.72
  220.2 2.9 fusion.72
  229.7 5.3 %collective-permute-start = (f32[256,256]{1,0:T(8,128)S(1)}, f32[256,256]{1,0:T(8,128)S(1)}, u32[]{:S(2)}, u32[]{:S(2)}) collective-permute-start(f32[256,256]{1,0:T(8,128)S(1)} %fusion.19), channel_id=1, source_target_pairs={{3,0},{4,1},{5,2},{6,3},{7,4},{8,5},{9,6},{10,7},{11,8},{12,9},{13... | collective-permute-start | bytes 786440 | tf_op jit(solution)/shard_map/ppermute | solution.py:41
  238.4 3.0 collective-permute-start.2
  251.5 6.3 %all-to-all-start.1 = ((f32[32,4,16,256]{3,2,1,0:T(8,128)}), f32[32,4,16,256]{3,2,1,0:T(8,128)S(1)}, u32[]{:S(2)}, u32[]{:S(2)}) async-start(f32[32,4,16,256]{3,2,1,0:T(8,128)} %copy.40), calls=%async_computation.1 | async-start | bytes 4194304 | tf_op jit(solution)/shard_map/all_to_all | solution.py:34
  259.1 6.1 %collective-permute-done.5 = f32[256,256]{1,0:T(8,128)} collective-permute-done((f32[256,256]{1,0:T(8,128)S(1)}, f32[256,256]{1,0:T(8,128)}, u32[]{:S(2)}, u32[]{:S(2)}) %collective-permute-start.5) | collective-permute-done | bytes 262176 | tf_op jit(solution)/shard_map/ppermute | solution.py:41
  269.1 11.7 %cholesky.49 = f32[128,128]{1,0:T(8,128)S(1)} custom-call(f32[128,128]{1,0:T(8,128)S(1)} %cholesky.115), custom_call_target="Cholesky" | custom-call | tf_op jit(solution)/shard_map/jit(cholesky)/cholesky | solution.py:116
  280.8 9.8 %custom-call.18 = f32[1,128,128]{1,2,0:T(8,128)S(1)} custom-call(f32[1,128,128]{2,1,0:T(8,128)S(1)} %get-tuple-element.261), custom_call_target="InvertDiagBlocksLowerTriangular" | custom-call | tf_op jit(solution)/shard_map/jit(cholesky)/cholesky | solution.py:116
  292.8 11.7 %cholesky.103 = f32[128,128]{1,0:T(8,128)S(1)} custom-call(f32[128,128]{1,0:T(8,128)S(1)} %convolution_subtract_fusion.1), custom_call_target="Cholesky" | custom-call | tf_op jit(solution)/shard_map/jit(cholesky)/cholesky | solution.py:116
  306.7 3.9 %while.17 = (s32[]{:T(128)}, f32[256,256]{1,0:T(8,128)S(1)}, s32[2,2]{1,0:T(2,128)S(1)}, f32[2,128,128]{2,1,0:T(8,128)S(1)}, s32[]{:T(128)}) while((s32[]{:T(128)}, f32[256,256]{1,0:T(8,128)S(1)}, s32[2,2]{1,0:T(2,128)S(1)}, f32[2,128,128]{2,1,0:T(8,128)S(1)}, s32[]{:T(128)}) %tuple.89), condition=%wide.while_cond, body=%wide.while_body.sunk | while | flops 2 | bytes 131181 | solution.py:118
  310.6 19.9 %custom-call.19 = f32[2,128,128]{1,2,0:T(8,128)S(1)} custom-call(f32[2,128,128]{2,1,0:T(8,128)S(1)} %get-tuple-element.165), custom_call_target="InvertDiagBlocksLowerTriangular" | custom-call | tf_op jit(solution)/shard_map/jit(_cho_solve)/triangular_solve | solution.py:118
  334.7 10.3 %all_gather.7 = f32[16,16,256]{2,1,0:T(8,128)S(1)} all-gather(f32[4,16,256]{2,1,0:T(8,128)S(1)} %reduce_sum.30), channel_id=1, replica_groups=mesh['grp'=4,'dev'=32] {'grp'}, dimensions={0}, use_global_device_ids=true | all-gather | bytes 327680 | tf_op jit(solution)/shard_map/all_gather | solution.py:125
  (198 shorter events, 91.6 us)
Async XLA Ops:
  7.2 16.2 %copy-start.3 = (f32[3,2048]{1,0:T(4,128)S(1)}, f32[3,2048]{1,0:T(4,128)}, u32[]{:S(2)}) copy-start(f32[3,2048]{1,0:T(4,128)} %param.7) | copy-start | bytes 73732
  7.2 11.5 %copy-start.4 = (s32[32]{0:T(128)S(1)}, s32[32]{0:T(128)}, u32[]{:S(2)}) copy-start(s32[32]{0:T(128)} %param.10) | copy-start | bytes 388
  7.2 15.4 %copy-start.5 = (s32[16]{0:T(128)S(1)}, s32[16]{0:T(128)}, u32[]{:S(2)}) copy-start(s32[16]{0:T(128)} %param.11) | copy-start | bytes 196
  7.2 124.0 %all-gather.2.cloned.1.call-start = ((), (), s32[]{:S(2)}) async-start(), calls=%async_computation.2 | async-start | bytes 34603008 | tf_op jit(solution)/shard_map/all_gather | solution.py:68
  9.9 30.0 %all-to-all-start = ((f32[32,3,2048]{2,1,0:T(4,128)}), f32[32,3,2048]{2,1,0:T(4,128)S(1)}, u32[]{:S(2)}, u32[]{:S(2)}) async-start(f32[32,3,2048]{2,1,0:T(4,128)} %broadcast_in_dim.127), calls=%async_computation | async-start | bytes 2097152 | tf_op jit(solution)/shard_map/all_to_all | solution.py:13
  131.2 103.8 %copy-start = (bf16[2048,256]{1,0:T(8,128)(2,1)S(1)}, bf16[2048,256]{1,0:T(8,128)(2,1)}, u32[]{:S(2)}) copy-start(bf16[2048,256]{1,0:T(8,128)(2,1)} %param.8) | copy-start | bytes 3145732
  229.7 17.2 %collective-permute-start = (f32[256,256]{1,0:T(8,128)S(1)}, f32[256,256]{1,0:T(8,128)S(1)}, u32[]{:S(2)}, u32[]{:S(2)}) collective-permute-start(f32[256,256]{1,0:T(8,128)S(1)} %fusion.19), channel_id=1, source_target_pairs={{3,0},{4,1},{5,2},{6,3},{7,4},{8,5},{9,6},{10,7},{11,8},{12,9},{13... | collective-permute-start | bytes 786440 | tf_op jit(solution)/shard_map/ppermute | solution.py:41
  236.0 21.9 %collective-permute-start.1 = (f32[256,256]{1,0:T(8,128)S(1)}, f32[256,256]{1,0:T(8,128)S(1)}, u32[]{:S(2)}, u32[]{:S(2)}) collective-permute-start(f32[256,256]{1,0:T(8,128)S(1)} %fusion.19), channel_id=1, source_target_pairs={{2,0},{3,1},{4,2},{5,3},{6,4},{7,5},{8,6},{9,7},{10,8},{11,9},{12,... | collective-permute-start | bytes 786440 | tf_op jit(solution)/shard_map/ppermute | solution.py:41
  238.4 19.4 %collective-permute-start.2 = (f32[256,256]{1,0:T(8,128)S(1)}, f32[256,256]{1,0:T(8,128)}, u32[]{:S(2)}, u32[]{:S(2)}) collective-permute-start(f32[256,256]{1,0:T(8,128)S(1)} %fusion.19), channel_id=1, source_target_pairs={{1,0},{2,1},{3,2},{4,3},{5,4},{6,5},{7,6},{8,7},{9,8},{10,9},{11,1... | collective-permute-start | bytes 786440 | tf_op jit(solution)/shard_map/ppermute | solution.py:41
  241.5 16.4 %collective-permute-start.3 = (f32[256,256]{1,0:T(8,128)S(1)}, f32[256,256]{1,0:T(8,128)}, u32[]{:S(2)}, u32[]{:S(2)}) collective-permute-start(f32[256,256]{1,0:T(8,128)S(1)} %fusion.19), channel_id=1, source_target_pairs={{0,1},{1,2},{2,3},{3,4},{4,5},{5,6},{6,7},{7,8},{8,9},{9,10},{10,1... | collective-permute-start | bytes 786440 | tf_op jit(solution)/shard_map/ppermute | solution.py:41
  244.0 15.1 %collective-permute-start.4 = (f32[256,256]{1,0:T(8,128)S(1)}, f32[256,256]{1,0:T(8,128)}, u32[]{:S(2)}, u32[]{:S(2)}) collective-permute-start(f32[256,256]{1,0:T(8,128)S(1)} %fusion.19), channel_id=1, source_target_pairs={{0,2},{1,3},{2,4},{3,5},{4,6},{5,7},{6,8},{7,9},{8,10},{9,11},{10,... | collective-permute-start | bytes 786440 | tf_op jit(solution)/shard_map/ppermute | solution.py:41
  246.8 18.4 %collective-permute-start.5 = (f32[256,256]{1,0:T(8,128)S(1)}, f32[256,256]{1,0:T(8,128)}, u32[]{:S(2)}, u32[]{:S(2)}) collective-permute-start(f32[256,256]{1,0:T(8,128)S(1)} %fusion.19), channel_id=1, source_target_pairs={{0,3},{1,4},{2,5},{3,6},{4,7},{5,8},{6,9},{7,10},{8,11},{9,12},{10... | collective-permute-start | bytes 786440 | tf_op jit(solution)/shard_map/ppermute | solution.py:41
  251.5 83.1 %all-to-all-start.1 = ((f32[32,4,16,256]{3,2,1,0:T(8,128)}), f32[32,4,16,256]{3,2,1,0:T(8,128)S(1)}, u32[]{:S(2)}, u32[]{:S(2)}) async-start(f32[32,4,16,256]{3,2,1,0:T(8,128)} %copy.40), calls=%async_computation.1 | async-start | bytes 4194304 | tf_op jit(solution)/shard_map/all_to_all | solution.py:34
  257.8 1.3 copy-start.2
  266.4 40.1 %copy-start.6 = (s32[2]{0:T(128)S(1)}, s32[2]{0:T(128)}, u32[]{:S(2)}) copy-start(s32[2]{0:T(128)} %iota_multiply_fusion) | copy-start | bytes 28
  268.4 0.7 copy-start.1
Sparse Core Ops, SparseCore 0:
  10.3 120.9 all-gather.1
where the time goes:
time: 355 us; the launch traced here: 353 us
  matrix products  100 us (28%)
  waiting for transfers between devices  66.5 us (19%)
  local copies, waits for them, and re-layouts  64.2 us (18%)
  other arithmetic  59.7 us (17%)
  starting transfers between devices  33.1 us (9%)
  between operations  17.2 us (5%)
  blocking collectives  10.3 us (3%)
    dot_general x32, matrix products, one_block(): return running + jnp.dot(kernel, sketch, preferred_element_type=jnp.float32)  92.2 us
    all_gather x1, waiting for transfers between devices, body(): piece = lax.all_gather(omega, 'dev', axis=0, tiled=True)  41.9 us
    another operation x6, other arithmetic, body(): factor = jnp.linalg.cholesky(gram_mat)  34 us
    unnamed x18, local copies, waits for them, and re-layouts  22.5 us
    another operation x3, other arithmetic, body(): interp = jax.scipy.linalg.cho_solve((factor, True), right_side.T).T  20.5 us
    ppermute x6, starting transfers between devices, shifted(): return lax.ppermute(block, axis, route)  18.5 us
    all_to_all x1, waiting for transfers between devices, copy_for_each(): return lax.all_to_all(copies, axis, split_axis=0, concat_axis=0, tiled=True)  16.6 us
    transpose x1, local copies, waits for them, and re-layouts, joined_along(): parts = jnp.moveaxis(parts, 0, dim)  15.4 us
  transfers between devices with their start and end apart: 9, of which 4 were waited for; matrix products, arithmetic and copies ran while one was open for 36% of the time, Pallas kernels for 0%

commit v1 on v0

--- a/solution.py
+++ b/solution.py
@@ -65,7 +65,8 @@
     my_leaf = slab_start // leaf_size
     slab_pts = lax.dynamic_slice_in_dim(every_point, slab_start, slab_rows, 1)
     start_sum = jnp.zeros((slab_rows, samples_n), jnp.float32)
-    piece = lax.all_gather(omega, "dev", axis=0, tiled=True)
+    repeated = jnp.stack([omega] * lax.axis_size("dev"))
+    piece = jnp.concatenate(lax.all_to_all(repeated, "dev", 0, 0), axis=0)
     piece_len = piece.shape[0]
     col_blk = math.gcd(piece_len, 2048)
 

time: 355 us -> 699 us (1.97); the launches traced: 353 us -> 690 us
  waiting for transfers between devices: 66.5 us -> 352 us
  starting transfers between devices: 33.1 us -> 64.2 us
  blocking collectives: 10.3 us -> 34.1 us
  between operations: 17.2 us -> 3.83 us
  local copies, waits for them, and re-layouts: 64.2 us -> 73 us
    all_to_all x1, waiting for transfers between devices: 16.6 us -> 352 us  [body(): piece = jnp.concatenate(lax.all_to_all(repeated, 'dev', 0, 0), axis=0)]
    all_gather x1 -> x0, waiting for transfers between devices: 41.9 us -> none  [body(): piece = lax.all_gather(omega, 'dev', axis=0, tiled=True)]
    ppermute x6, starting transfers between devices: 18.5 us -> 47.8 us  [shifted(): return lax.ppermute(block, axis, route)]
    all_to_all x0 -> x1, blocking collectives: none -> 23.7 us  [copy_for_each(): return lax.all_to_all(copies, axis, split_axis=0, concat_axis=0, tiled=True)]
    another operation x6 -> x7, local copies, waits for them, and re-layouts: 3.9 us -> 16.1 us  [the longest x1 10.9 us: body(): repeated = jnp.stack([omega] * lax.axis_size('dev'))]
    ppermute x6, waiting for transfers between devices: 7.35 us -> 0.02 us  [shifted(): return lax.ppermute(block, axis, route)]
    unnamed x18 -> x14, local copies, waits for them, and re-layouts: 22.5 us -> 20.5 us
  transfers between devices with their start and end apart: 9 -> 8, of which waited for: 4 -> 1; matrix products, arithmetic and copies ran while one was open for 36% -> 18% of each run, Pallas kernels for 0% -> 0%
where the time goes in v1:
time: 699 us; the launch traced here: 690 us
  waiting for transfers between devices  352 us (50%)
  matrix products  100 us (14%)
  local copies, waits for them, and re-layouts  73 us (10%)
  starting transfers between devices  64.2 us (9%)
  other arithmetic  60.5 us (9%)
  blocking collectives  34.1 us (5%)
    all_to_all x1, waiting for transfers between devices, body(): piece = jnp.concatenate(lax.all_to_all(repeated, 'dev', 0, 0), axis=0)  352 us
    dot_general x32, matrix products, one_block(): return running + jnp.dot(kernel, sketch, preferred_element_type=jnp.float32)  92.1 us
    ppermute x6, starting transfers between devices, shifted(): return lax.ppermute(block, axis, route)  47.8 us
    another operation x6, other arithmetic, body(): factor = jnp.linalg.cholesky(gram_mat)  34 us
    all_to_all x1, blocking collectives, copy_for_each(): return lax.all_to_all(copies, axis, split_axis=0, concat_axis=0, tiled=True)  23.7 us
    another operation x3, other arithmetic, body(): interp = jax.scipy.linalg.cho_solve((factor, True), right_side.T).T  20.5 us
    unnamed x14, local copies, waits for them, and re-layouts  20.5 us
    transpose x1, local copies, waits for them, and re-layouts, joined_along(): parts = jnp.moveaxis(parts, 0, dim)  15.4 us
  transfers between devices with their start and end apart: 8, of which 1 were waited for; matrix products, arithmetic and copies ran while one was open for 18% of the time, Pallas kernels for 0%

profile of v1, /device:TPU:33, one launch (start us, length us, event | category | flops | bytes accessed | tf_op | source)
XLA Modules:
  0.0 689.9 jit_solution(16369430782688764849)
XLA Ops:
  1.7 23.7 %all_to_all.15 = f32[32,3,2048]{2,1,0:T(4,128)S(1)} all-to-all(f32[32,3,2048]{2,1,0:T(4,128)S(1)} %broadcast_in_dim.127), channel_id=1, replica_groups=mesh['grp'=4,'dev'=32] {'dev'}, dimensions={0} | all-to-all | bytes 1572864 | tf_op jit(solution)/shard_map/all_to_all | solution.py:13
  25.4 10.9 %stack.2 = bf16[32,2048,256]{2,1,0:T(8,128)(2,1)} broadcast(bf16[2048,256]{1,0:T(8,128)(2,1)S(1)} %copy-done), dimensions={1,2} | broadcast | bytes 34603008 | tf_op jit(solution)/shard_map/stack | solution.py:68
  36.3 7.3 %all-to-all-start.1 = ((bf16[32,2048,256]{2,1,0:T(8,128)(2,1)}), bf16[32,2048,256]{2,1,0:T(8,128)(2,1)}, u32[]{:S(2)}, u32[]{:S(2)}) async-start(bf16[32,2048,256]{2,1,0:T(8,128)(2,1)} %stack.2), calls=%async_computation.1 | async-start | bytes 67108864 | tf_op jit(solution)/shard_map/all_to_all | solution.py:69
  48.4 15.4 %copy.36 = f32[3,32,2048]{0,2,1:T(8,128)} copy(f32[3,32,2048]{2,0,1:T(4,128)S(1)} %bitcast.90) | data formatting | bytes 1572864 | tf_op jit(solution)/shard_map/transpose | solution.py:17
  63.8 18.0 %copy.38 = f32[3,65536]{1,0:T(4,128)S(1)} copy(f32[3,65536]{0,1:T(8,128)} %bitcast.85) | data formatting | bytes 1572864
  81.8 11.3 %gather_fusion = f32[256,3]{1,0:T(8,128)S(1)} fusion(f32[3,65536]{0,1:T(8,128)} %bitcast.86, s32[1024]{0:T(1024)S(1)} %pad_clamp_fusion), kind=kCustom, calls=%fused_computation | custom fusion | bytes 7168 | tf_op jit(solution)/shard_map/gather | solution.py:93
  94.4 352.5 %all-to-all-done.1 = bf16[32,2048,256]{2,1,0:T(8,128)(2,1)} async-done(((bf16[32,2048,256]{2,1,0:T(8,128)(2,1)}), bf16[32,2048,256]{2,1,0:T(8,128)(2,1)}, u32[]{:S(2)}, u32[]{:S(2)}) %all-to-all-start.1) | async-done | bytes 33554464 | tf_op jit(solution)/shard_map/all_to_all | solution.py:69
  446.9 97.9 %while.18 = (s32[]{:T(128)}, f32[512,256]{1,0:T(8,128)S(1)}, s32[]{:T(128)}, f32[3,512]{1,0:T(4,128)S(1)}, f32[3,65536]{1,0:T(4,128)S(1)}, /*index=5*/bf16[65536...) while((s32[]{:T(128)}, f32[512,256]{1,0:T(8,128)S(1)}, ...), condition=%wide.region_1.2_spmd.clone, body=%wide.region_0.1_spmd.clone.sunk | while | flops 548702208 | bytes 2193629 | solution.py:82
  453.2 2.9 fusion.72
  456.2 2.9 fusion.72
  462.4 2.9 fusion.72
  465.4 2.9 fusion.72
  474.6 2.9 fusion.72
  477.6 2.9 fusion.72
  483.8 2.9 fusion.72
  496.0 2.9 fusion.72
  505.2 2.9 fusion.72
  517.4 2.9 fusion.72
  529.7 2.9 fusion.72
  541.9 2.9 fusion.72
  545.3 22.6 %collective-permute-start = (f32[256,256]{1,0:T(8,128)S(1)}, f32[256,256]{1,0:T(8,128)S(1)}, u32[]{:S(2)}, u32[]{:S(2)}) collective-permute-start(f32[256,256]{1,0:T(8,128)S(1)} %fusion.19), channel_id=1, source_target_pairs={{3,0},{4,1},{5,2},{6,3},{7,4},{8,5},{9,6},{10,7},{11,8},{12,9},{13... | collective-permute-start | bytes 786440 | tf_op jit(solution)/shard_map/ppermute | solution.py:41
  568.8 4.6 collective-permute-start.1
  575.3 3.6 collective-permute-start.3
  578.9 10.3 %collective-permute-start.4 = (f32[256,256]{1,0:T(8,128)S(1)}, f32[256,256]{1,0:T(8,128)}, u32[]{:S(2)}, u32[]{:S(2)}) collective-permute-start(f32[256,256]{1,0:T(8,128)S(1)} %fusion.19), channel_id=1, source_target_pairs={{0,2},{1,3},{2,4},{3,5},{4,6},{5,7},{6,8},{7,9},{8,10},{9,11},{10,... | collective-permute-start | bytes 786440 | tf_op jit(solution)/shard_map/ppermute | solution.py:41
  589.3 4.7 collective-permute-start.5
  596.4 9.2 %all-to-all-start.2 = ((f32[32,4,16,256]{3,2,1,0:T(8,128)}), f32[32,4,16,256]{3,2,1,0:T(8,128)S(1)}, u32[]{:S(2)}, u32[]{:S(2)}) async-start(f32[32,4,16,256]{3,2,1,0:T(8,128)} %copy.40), calls=%async_computation.2 | async-start | bytes 4194304 | tf_op jit(solution)/shard_map/all_to_all | solution.py:34
  611.0 11.7 %cholesky.49 = f32[128,128]{1,0:T(8,128)S(1)} custom-call(f32[128,128]{1,0:T(8,128)S(1)} %cholesky.115), custom_call_target="Cholesky" | custom-call | tf_op jit(solution)/shard_map/jit(cholesky)/cholesky | solution.py:117
  622.8 9.8 %custom-call.18 = f32[1,128,128]{1,2,0:T(8,128)S(1)} custom-call(f32[1,128,128]{2,1,0:T(8,128)S(1)} %get-tuple-element.261), custom_call_target="InvertDiagBlocksLowerTriangular" | custom-call | tf_op jit(solution)/shard_map/jit(cholesky)/cholesky | solution.py:117
  634.8 11.7 %cholesky.103 = f32[128,128]{1,0:T(8,128)S(1)} custom-call(f32[128,128]{1,0:T(8,128)S(1)} %convolution_subtract_fusion.1), custom_call_target="Cholesky" | custom-call | tf_op jit(solution)/shard_map/jit(cholesky)/cholesky | solution.py:117
  648.5 5.2 while.17
  653.7 20.5 %custom-call.19 = f32[2,128,128]{1,2,0:T(8,128)S(1)} custom-call(f32[2,128,128]{2,1,0:T(8,128)} %get-tuple-element.165), custom_call_target="InvertDiagBlocksLowerTriangular" | custom-call | tf_op jit(solution)/shard_map/jit(_cho_solve)/triangular_solve | solution.py:119
  678.4 10.4 %all_gather.3 = f32[16,16,256]{2,1,0:T(8,128)S(1)} all-gather(f32[4,16,256]{2,1,0:T(8,128)S(1)} %reduce_sum.30), channel_id=1, replica_groups=mesh['grp'=4,'dev'=32] {'grp'}, dimensions={0}, use_global_device_ids=true | all-gather | bytes 327680 | tf_op jit(solution)/shard_map/all_gather | solution.py:126
  (193 shorter events, 91.6 us)
Async XLA Ops:
  0.6 24.8 %copy-start = (bf16[2048,256]{1,0:T(8,128)(2,1)S(1)}, bf16[2048,256]{1,0:T(8,128)(2,1)}, u32[]{:S(2)}) copy-start(bf16[2048,256]{1,0:T(8,128)(2,1)} %param.8) | copy-start | bytes 3145732
  36.3 7.8 %copy-start.3 = (s32[32]{0:T(128)S(1)}, s32[32]{0:T(128)}, u32[]{:S(2)}) copy-start(s32[32]{0:T(128)} %param.10) | copy-start | bytes 388
  36.3 11.9 %copy-start.4 = (s32[16]{0:T(128)S(1)}, s32[16]{0:T(128)}, u32[]{:S(2)}) copy-start(s32[16]{0:T(128)} %param.11) | copy-start | bytes 196
  36.3 12.1 %copy-start.2 = (f32[3,2048]{1,0:T(4,128)S(1)}, f32[3,2048]{1,0:T(4,128)}, u32[]{:S(2)}) copy-start(f32[3,2048]{1,0:T(4,128)} %param.7) | copy-start | bytes 73732
  36.3 410.6 %all-to-all-start.1 = ((bf16[32,2048,256]{2,1,0:T(8,128)(2,1)}), bf16[32,2048,256]{2,1,0:T(8,128)(2,1)}, u32[]{:S(2)}, u32[]{:S(2)}) async-start(bf16[32,2048,256]{2,1,0:T(8,128)(2,1)} %stack.2), calls=%async_computation.1 | async-start | bytes 67108864 | tf_op jit(solution)/shard_map/all_to_all | solution.py:69
  545.3 44.0 %collective-permute-start = (f32[256,256]{1,0:T(8,128)S(1)}, f32[256,256]{1,0:T(8,128)S(1)}, u32[]{:S(2)}, u32[]{:S(2)}) collective-permute-start(f32[256,256]{1,0:T(8,128)S(1)} %fusion.19), channel_id=1, source_target_pairs={{3,0},{4,1},{5,2},{6,3},{7,4},{8,5},{9,6},{10,7},{11,8},{12,9},{13... | collective-permute-start | bytes 786440 | tf_op jit(solution)/shard_map/ppermute | solution.py:41
  568.8 36.8 %collective-permute-start.1 = (f32[256,256]{1,0:T(8,128)S(1)}, f32[256,256]{1,0:T(8,128)S(1)}, u32[]{:S(2)}, u32[]{:S(2)}) collective-permute-start(f32[256,256]{1,0:T(8,128)S(1)} %fusion.19), channel_id=1, source_target_pairs={{2,0},{3,1},{4,2},{5,3},{6,4},{7,5},{8,6},{9,7},{10,8},{11,9},{12,... | collective-permute-start | bytes 786440 | tf_op jit(solution)/shard_map/ppermute | solution.py:41
  573.4 32.3 %collective-permute-start.2 = (f32[256,256]{1,0:T(8,128)S(1)}, f32[256,256]{1,0:T(8,128)}, u32[]{:S(2)}, u32[]{:S(2)}) collective-permute-start(f32[256,256]{1,0:T(8,128)S(1)} %fusion.19), channel_id=1, source_target_pairs={{1,0},{2,1},{3,2},{4,3},{5,4},{6,5},{7,6},{8,7},{9,8},{10,9},{11,1... | collective-permute-start | bytes 786440 | tf_op jit(solution)/shard_map/ppermute | solution.py:41
  575.3 30.3 %collective-permute-start.3 = (f32[256,256]{1,0:T(8,128)S(1)}, f32[256,256]{1,0:T(8,128)}, u32[]{:S(2)}, u32[]{:S(2)}) collective-permute-start(f32[256,256]{1,0:T(8,128)S(1)} %fusion.19), channel_id=1, source_target_pairs={{0,1},{1,2},{2,3},{3,4},{4,5},{5,6},{6,7},{7,8},{8,9},{9,10},{10,1... | collective-permute-start | bytes 786440 | tf_op jit(solution)/shard_map/ppermute | solution.py:41
  578.9 26.7 %collective-permute-start.4 = (f32[256,256]{1,0:T(8,128)S(1)}, f32[256,256]{1,0:T(8,128)}, u32[]{:S(2)}, u32[]{:S(2)}) collective-permute-start(f32[256,256]{1,0:T(8,128)S(1)} %fusion.19), channel_id=1, source_target_pairs={{0,2},{1,3},{2,4},{3,5},{4,6},{5,7},{6,8},{7,9},{8,10},{9,11},{10,... | collective-permute-start | bytes 786440 | tf_op jit(solution)/shard_map/ppermute | solution.py:41
  589.3 17.0 %collective-permute-start.5 = (f32[256,256]{1,0:T(8,128)S(1)}, f32[256,256]{1,0:T(8,128)}, u32[]{:S(2)}, u32[]{:S(2)}) collective-permute-start(f32[256,256]{1,0:T(8,128)S(1)} %fusion.19), channel_id=1, source_target_pairs={{0,3},{1,4},{2,5},{3,6},{4,7},{5,8},{6,9},{7,10},{8,11},{9,12},{10... | collective-permute-start | bytes 786440 | tf_op jit(solution)/shard_map/ppermute | solution.py:41
  596.4 81.9 %all-to-all-start.2 = ((f32[32,4,16,256]{3,2,1,0:T(8,128)}), f32[32,4,16,256]{3,2,1,0:T(8,128)S(1)}, u32[]{:S(2)}, u32[]{:S(2)}) async-start(f32[32,4,16,256]{3,2,1,0:T(8,128)} %copy.40), calls=%async_computation.2 | async-start | bytes 4194304 | tf_op jit(solution)/shard_map/all_to_all | solution.py:34
  605.6 0.7 copy-start.1
